TPU v7x, 32 devices: a whole 2x2x4 slice. The times are simulated.
32 devices in a mesh: seq: 8 (over z, x), chan: 4 (over y, core).
Axes of the slice: x: 2, y: 2, z: 4, core: 2. Of those that a mesh axis runs over, the one named last changes fastest.
Arguments:
- values: bfloat16 [2048, 4096], P('seq', 'chan'), may hold values from -6 to 6
- gates: bfloat16 [2048, 4096], P('seq', 'chan'), may hold values from -6 to 6
- filters: float32 [2048, 4096], P('seq', 'chan'), may hold values from -4 to 4
- skip: float32 [4096], P('chan'), may hold values from -1 to 1
- w_out: bfloat16 [4096, 4096], P(None, 'chan'), may hold values from -0.09375 to 0.09375
Outputs:
- output: bfloat16 [2048, 4096], P('seq', 'chan')
All inputs are finite; a program needn't handle non-finite values.
Results may differ from a plain program's by a relative error of at most 0.0056.
Values may be sent and summed in bfloat16 or wider, within the bound.
A program may use at most 128 MiB of HBM per device.

v0:
```python
import functools
import math

import jax
import jax.numpy as jnp
import numpy as np
from jax import lax
from jax.experimental import pallas as pl
from jax.experimental.pallas import tpu as pltpu
from jax.sharding import PartitionSpec as P

LANES = 128
STRIP = 16
IN_PARTS = 2
OUT_PARTS = 4
MESH = pl.DeviceIdType.MESH


def product(form, left, right):
    return jnp.einsum(
        form, left, right, precision=lax.Precision.HIGHEST, preferred_element_type=jnp.float32
    )


def phase(first_count, second_count, modulus):
    left = lax.iota(jnp.int32, first_count)[:, None]
    right = lax.iota(jnp.int32, second_count)[None, :]
    angle = (left * right % modulus).astype(jnp.float32) * (2.0 * math.pi / modulus)
    return (jnp.cos(angle), jnp.sin(angle))


def spectral_conv(chan_values, chan_filter):
    nchan = chan_values.shape[0]
    length = chan_values.shape[1]
    summed = 2 * length
    columns = 128
    row_count = summed // columns
    half_rows = row_count // 2
    cos_rows, sin_rows = phase(row_count, half_rows, row_count)
    cos_twist, sin_twist = phase(row_count, columns, summed)
    cos_cols, sin_cols = phase(columns, columns, columns)
    cos_back, sin_back = phase(half_rows, row_count, row_count)

    def forward(signal):
        grid = signal.astype(jnp.float32).reshape(nchan, half_rows, columns)
        real_a = product("kn,cna->cka", cos_rows, grid)
        imag_a = -product("kn,cna->cka", sin_rows, grid)
        real_b = real_a * cos_twist + imag_a * sin_twist
        imag_b = imag_a * cos_twist - real_a * sin_twist
        real_c = product("cka,am->ckm", real_b, cos_cols) + product("cka,am->ckm", imag_b, sin_cols)
        imag_c = product("cka,am->ckm", imag_b, cos_cols) - product("cka,am->ckm", real_b, sin_cols)
        return (real_c, imag_c)

    real_v, imag_v = forward(chan_values)
    real_h, imag_h = forward(chan_filter)
    real_p = real_v * real_h - imag_v * imag_h
    imag_p = real_v * imag_h + imag_v * real_h
    real_d = product("ckm,ma->cka", real_p, cos_cols) - product("ckm,ma->cka", imag_p, sin_cols)
    imag_d = product("ckm,ma->cka", imag_p, cos_cols) + product("ckm,ma->cka", real_p, sin_cols)
    real_e = real_d * cos_twist - imag_d * sin_twist
    imag_e = imag_d * cos_twist + real_d * sin_twist
    result = product("nk,cka->cna", cos_back, real_e) - product("nk,cka->cna", sin_back, imag_e)
    return (result * (1.0 / summed)).reshape(nchan, length).astype(jnp.bfloat16)


def per_device_generic(values, gates, filters, skip, w_out):
    value_trans = values.T
    filter_trans = filters.T
    chan_values = lax.all_to_all(value_trans, "seq", split_axis=0, concat_axis=1, tiled=True)
    chan_filter = lax.all_to_all(filter_trans, "seq", split_axis=0, concat_axis=1, tiled=True)
    convolved = spectral_conv(chan_values, chan_filter)
    causal_trans = lax.all_to_all(convolved, "seq", split_axis=1, concat_axis=0, tiled=True)
    causal = causal_trans.T
    mixed = (
        gates.astype(jnp.float32)
        * (causal.astype(jnp.float32) + skip[None, :] * values.astype(jnp.float32))
    ).astype(jnp.bfloat16)
    projected = jnp.dot(
        lax.all_gather(mixed, "chan", axis=1, tiled=True), w_out, preferred_element_type=jnp.float32
    )
    return projected.astype(jnp.bfloat16)


def split(x):
    high = x.astype(jnp.bfloat16)
    return high, (x - high.astype(jnp.float32)).astype(jnp.bfloat16)


def tables(blocks, block, parts):
    index = np.arange(block)
    angle = 2.0 * np.pi * (np.outer(index, index) % block) / block
    cos, sin = np.cos(angle), np.sin(angle)
    whole = np.block([[cos, sin], [-sin, cos]]).astype(np.float32)
    high = whole.astype(jnp.bfloat16)
    both = np.stack([high, (whole - high.astype(np.float32)).astype(jnp.bfloat16)])

    def members(count):
        size = block // count
        return [np.concatenate([index[p * size : (p + 1) * size] + block * i for i in (0, 1)]) for p in range(count)]

    forward = np.stack([both[:, :, m] for m in members(IN_PARTS)])
    backward = np.stack([both[:, m, :] for m in members(parts)])
    turn = 2.0 * np.pi * np.outer(index, np.arange(blocks) + 0.5) / (2 * blocks * block)
    twiddle = np.zeros((block, LANES), np.float32)
    twiddle[:, :blocks] = np.cos(turn)
    twiddle[:, blocks : 2 * blocks] = np.sin(turn)
    return forward, backward, twiddle


def weighted(terms):
    total = None
    for weight, term in terms:
        part = term if weight == 1.0 else term * np.float32(weight)
        total = part if total is None else total + part
    return total


def kernel(
    blocks, chans, parts,
    values_hbm, gates_hbm, filters_hbm, skip, forward_hbm, backward_hbm, twiddle, w_hbm,
    out,
    values, gates, filters, h_send, got_v, got_h, forward, backward, z, spec_v, spec_h, y, d, y_send, causal, mixed, w, acc,
    l_sem, v_out, v_in, h_out, h_in, c_out, c_in, a_out, a_in, b_out, b_in, f_out, f_in,
):
    me = lax.axis_index("seq")
    mine = lax.axis_index("chan")
    block = values.shape[0]
    half = blocks // 2
    piece = block // IN_PARTS
    chunk = block // parts

    def columns(position):
        return pl.ds(pl.multiple_of(position * LANES, LANES), LANES)

    def ahead(step):
        return lax.rem(me + step, blocks)

    def behind(step):
        return lax.rem(me + blocks - step, blocks)

    local = [
        pltpu.make_async_copy(source, target, l_sem.at[i])
        for i, (source, target) in enumerate((
            (filters_hbm, filters), (values_hbm, values), (values_hbm.at[:, columns(me)], got_v.at[me]),
            (forward_hbm, forward), (backward_hbm, backward), (gates_hbm, gates), (w_hbm, w),
        ))
    ]
    filters_copy, values_copy, own_copy, forward_copy, backward_copy, gates_copy, w_copy = local
    for copy in local:
        copy.start()

    sibling = mine + 1 - 2 * lax.rem(mine, 2)
    across = lax.rem(mine + 2, chans)
    barrier = pltpu.get_barrier_semaphore()
    for step in range(1, blocks):
        pl.semaphore_signal(barrier, inc=1, device_id={"seq": ahead(step)}, device_id_type=MESH)
    for other in (sibling, across):
        pl.semaphore_signal(barrier, inc=1, device_id={"chan": other}, device_id_type=MESH)
    pl.semaphore_wait(barrier, blocks + 1)

    def exchange(source, target, out_sem, in_sem, part, step):
        rows = pl.ds(part * piece, piece)
        return pltpu.make_async_remote_copy(
            src_ref=source.at[rows, columns(ahead(step))],
            dst_ref=target.at[me, rows],
            send_sem=out_sem.at[part, step],
            recv_sem=in_sem.at[part, step],
            device_id={"seq": ahead(step)},
            device_id_type=MESH,
        )

    order = sorted(range(1, blocks), key=lambda step: -min(step, blocks - step))
    v_copies = [[exchange(values_hbm, got_v, v_out, v_in, part, step) for step in order] for part in range(IN_PARTS)]
    for copies in v_copies:
        for copy in copies:
            copy.start()
    filters_copy.wait()
    h_copies = [[exchange(h_send, got_h, h_out, h_in, part, step) for step in order] for part in range(IN_PARTS)]
    for part in range(IN_PARTS):
        rows = pl.ds(part * piece, piece)
        h_send[rows, :] = filters[rows, :].astype(jnp.bfloat16)
        for copy in h_copies[part]:
            copy.start()
    got_h[me] = h_send[:, columns(me)]
    own_copy.wait()
    forward_copy.wait()

    def spread(got, part):
        def body(strip, _):
            here = pl.multiple_of(strip * STRIP, STRIP)
            rows = pl.ds(part * piece + here, STRIP)
            x = [got[n, rows, :].astype(jnp.float32) for n in range(blocks)]
            for r in range(half):
                phi = math.pi * (2 * r + 1) / (2 * blocks)
                sums = []
                for odd in (0, 1):
                    picks = range(odd, blocks, 2)
                    sums.append(weighted([(math.cos(phi * n), x[n]) for n in picks]))
                    sums.append(weighted([(-math.sin(phi * n), x[n]) for n in picks if n]))
                even_re, even_im, odd_re, odd_im = sums
                for res, re, im in (
                    (r, even_re + odd_re, even_im + odd_im),
                    (blocks - 1 - r, even_re - odd_re, odd_im - even_im),
                ):
                    cos = twiddle[rows, res : res + 1]
                    sin = twiddle[rows, blocks + res : blocks + res + 1]
                    lanes = slice(res % 2 * LANES, (res % 2 + 1) * LANES)
                    re_high, re_low = split(re * cos + im * sin)
                    im_high, im_low = split(im * cos - re * sin)
                    for place, value in enumerate((re_high, im_high, re_low, im_low)):
                        z[res // 2, pl.ds(place * piece + here, STRIP), lanes] = value
            return 0

        lax.fori_loop(0, piece // STRIP, body, 0)

    def times(high, low, x):
        middle = x.shape[0] // 2
        return (
            jnp.dot(high, x[:middle], preferred_element_type=jnp.float32)
            + jnp.dot(low, x[:middle], preferred_element_type=jnp.float32)
            + jnp.dot(high, x[middle:], preferred_element_type=jnp.float32)
        )

    def transform(spectrum, part):
        def body(pair, _):
            x = times(forward[part, 0], forward[part, 1], z[pair])
            spectrum[pair] = spectrum[pair] + x if part else x
            return 0

        lax.fori_loop(0, half, body, 0)

    for got, copies, spectrum in ((got_v, v_copies, spec_v), (got_h, h_copies, spec_h)):
        for part in range(IN_PARTS):
            for copy in copies[part]:
                copy.wait_recv()
            spread(got, part)
            transform(spectrum, part)

    def product(pair, _):
        re_v, re_h = spec_v[pair, :block], spec_h[pair, :block]
        im_v, im_h = spec_v[pair, block:], spec_h[pair, block:]
        re_high, re_low = split(re_v * re_h - im_v * im_h)
        im_high, im_low = split(-(re_v * im_h + im_v * re_h))
        for place, value in enumerate((re_high, im_high, re_low, im_low)):
            y[pair, place * block : (place + 1) * block] = value
        return 0

    lax.fori_loop(0, half, product, 0)
    backward_copy.wait()

    def undo(part):
        def inverse(pair, _):
            d[pair] = times(backward[part, 0], backward[part, 1], y[pair])
            return 0

        lax.fori_loop(0, half, inverse, 0)

        def body(strip, _):
            here = pl.multiple_of(strip * STRIP, STRIP)
            rows = pl.ds(part * chunk + here, STRIP)
            scale = 1.0 / (blocks * block)
            sums = []
            for r in range(half):
                turned = []
                for res in (r, blocks - 1 - r):
                    lanes = slice(res % 2 * LANES, (res % 2 + 1) * LANES)
                    re = d[res // 2, pl.ds(here, STRIP), lanes]
                    im = -d[res // 2, pl.ds(chunk + here, STRIP), lanes]
                    cos = twiddle[rows, res : res + 1]
                    sin = twiddle[rows, blocks + res : blocks + res + 1]
                    turned.append((re * cos - im * sin, im * cos + re * sin))
                (re_a, im_a), (re_b, im_b) = turned
                sums.append(((re_a + re_b, im_a - im_b), (re_a - re_b, im_a + im_b)))
            for n in range(blocks):
                terms = []
                for r in range(half):
                    phi = math.pi * (2 * r + 1) / (2 * blocks)
                    re, im = sums[r][n % 2]
                    terms.append((scale * math.cos(phi * n), re))
                    if n:
                        terms.append((-scale * math.sin(phi * n), im))
                y_send[n, rows, :] = weighted(terms).astype(jnp.bfloat16)
            return 0

        lax.fori_loop(0, chunk // STRIP, body, 0)

    c_copies = []
    for part in range(parts):
        undo(part)
        rows = pl.ds(part * chunk, chunk)
        c_copies.append([
            pltpu.make_async_remote_copy(
                src_ref=y_send.at[ahead(step), rows],
                dst_ref=causal.at[me, rows],
                send_sem=c_out.at[part, step],
                recv_sem=c_in.at[part, step],
                device_id={"seq": ahead(step)},
                device_id_type=MESH,
            )
            for step in order
        ])
        for copy in c_copies[part]:
            copy.start()
        causal[me, rows] = y_send[me, rows]

    def share(source_chan, target, out_sem, in_sem, part):
        spot = mixed.at[source_chan, pl.ds(part * chunk, chunk)]
        return pltpu.make_async_remote_copy(
            src_ref=spot, dst_ref=spot,
            send_sem=out_sem.at[part], recv_sem=in_sem.at[part],
            device_id={"chan": target}, device_id_type=MESH,
        )

    depth = values.shape[1]
    a_copies = [share(mine, across, a_out, a_in, part) for part in range(parts)]
    b_copies = [share(mine, sibling, b_out, b_in, part) for part in range(parts)]
    f_copies = [share(across, sibling, f_out, f_in, part) for part in range(parts)]
    opposite = lax.rem(sibling + 2, chans)

    def blend(part):
        rows = pl.ds(part * chunk, chunk)
        for source in range(blocks):
            cols = slice(source * LANES, (source + 1) * LANES)
            direct = skip[:, cols] * values[rows, cols].astype(jnp.float32)
            mixed[mine, rows, cols] = (
                gates[rows, cols].astype(jnp.float32) * (causal[source, rows].astype(jnp.float32) + direct)
            ).astype(jnp.bfloat16)

    def project(part, pair, last):
        rows = pl.ds(part * chunk, chunk)

        def tile(n, _):
            cols = pl.ds(pl.multiple_of(n * 256, 256), 256)
            total = None
            for which in pair:
                deep = pl.ds(pl.multiple_of(which * depth, depth), depth)
                term = jnp.dot(mixed[which, rows], w[deep, cols], preferred_element_type=jnp.float32)
                total = term if total is None else total + term
            if last:
                out[rows, cols] = (total + acc[rows, cols]).astype(out.dtype)
            else:
                acc[rows, cols] = total
            return 0

        lax.fori_loop(0, out.shape[1] // 256, tile, 0)

    def finish(part):
        f_copies[part].wait_recv()
        project(part, (across, opposite), True)

    values_copy.wait()
    gates_copy.wait()
    w_copy.wait()
    for part in range(parts):
        for copy in c_copies[part]:
            copy.wait_recv()
        blend(part)
        a_copies[part].start()
        b_copies[part].start()
        if part >= 1:
            a_copies[part - 1].wait_recv()
            f_copies[part - 1].start()
        b_copies[part].wait_recv()
        project(part, (mine, sibling), False)
        if part >= 1 and part < parts - 1:
            finish(part - 1)
    a_copies[parts - 1].wait_recv()
    f_copies[parts - 1].start()
    if parts >= 2:
        finish(parts - 2)
    finish(parts - 1)
    for copies in v_copies + h_copies + c_copies + [a_copies, b_copies, f_copies]:
        for copy in copies:
            copy.wait_send()


def per_device_fused(blocks, chans, values, gates, filters, skip, w_out):
    block, width = values.shape
    parts = OUT_PARTS
    forward, backward, twiddle = tables(blocks, block, parts)
    vmem = pl.BlockSpec(memory_space=pltpu.VMEM)
    hbm = pl.BlockSpec(memory_space=pl.ANY)
    half = blocks // 2
    out_width = w_out.shape[1]

    def sems(*shape):
        return pltpu.SemaphoreType.DMA(shape)

    return pl.pallas_call(
        functools.partial(kernel, blocks, chans, parts),
        out_shape=jax.ShapeDtypeStruct((block, out_width), jnp.bfloat16),
        in_specs=[hbm, hbm, hbm, vmem, hbm, hbm, vmem, hbm],
        out_specs=vmem,
        scratch_shapes=[
            pltpu.VMEM((block, width), jnp.bfloat16),
            pltpu.VMEM((block, width), jnp.bfloat16),
            pltpu.VMEM((block, width), jnp.float32),
            pltpu.VMEM((block, width), jnp.bfloat16),
            pltpu.VMEM((blocks, block, LANES), jnp.bfloat16),
            pltpu.VMEM((blocks, block, LANES), jnp.bfloat16),
            pltpu.VMEM(forward.shape, jnp.bfloat16),
            pltpu.VMEM(backward.shape, jnp.bfloat16),
            pltpu.VMEM((half, 4 * block // IN_PARTS, 2 * LANES), jnp.bfloat16),
            pltpu.VMEM((half, 2 * block, 2 * LANES), jnp.float32),
            pltpu.VMEM((half, 2 * block, 2 * LANES), jnp.float32),
            pltpu.VMEM((half, 4 * block, 2 * LANES), jnp.bfloat16),
            pltpu.VMEM((half, 2 * block // parts, 2 * LANES), jnp.float32),
            pltpu.VMEM((blocks, block, LANES), jnp.bfloat16),
            pltpu.VMEM((blocks, block, LANES), jnp.bfloat16),
            pltpu.VMEM((chans, block, width), jnp.bfloat16),
            pltpu.VMEM(w_out.shape, jnp.bfloat16),
            pltpu.VMEM((block, out_width), jnp.float32),
            sems(7),
        ]
        + [sems(IN_PARTS, blocks)] * 4
        + [sems(parts, blocks)] * 2
        + [sems(parts)] * 6,
        compiler_params=pltpu.CompilerParams(
            collective_id=0, has_side_effects=True, vmem_limit_bytes=56 * 2**20
        ),
    )(values, gates, filters, skip[None, :], jnp.asarray(forward), jnp.asarray(backward), jnp.asarray(twiddle), w_out)


def per_device(mesh_shape, values, gates, filters, skip, w_out):
    blocks, chans = mesh_shape["seq"], mesh_shape["chan"]
    block, width = values.shape
    fits = (
        width == blocks * LANES and chans == 4 and blocks % 2 == 0 and blocks <= 16
        and block % 256 == 0 and block <= 512 and w_out.shape[1] % 256 == 0
    )
    if fits:
        return per_device_fused(blocks, chans, values, gates, filters, skip, w_out)
    return per_device_generic(values, gates, filters, skip, w_out)


def solution(mesh):
    placed = (P("seq", "chan"), P("seq", "chan"), P("seq", "chan"), P("chan"), P(None, "chan"))
    return jax.shard_map(
        functools.partial(per_device, dict(mesh.shape)),
        mesh=mesh, in_specs=placed, out_specs=P("seq", "chan"), check_vma=False,
    )
```

profile of v0, /device:TPU:0, one launch (start us, length us, event | category | flops | bytes accessed | tf_op | source)
XLA Modules:
  0.0 63.9 jit_solution(7283512712761157992)
XLA Ops:
  0.0 62.0 %shard_map.82 = bf16[256,1024]{1,0:T(8,128)(2,1)} custom-call(bf16[256,1024]{1,0:T(8,128)(2,1)} %values_hbm.1, bf16[256,1024]{1,0:T(8,128)(2,1)} %gates_hbm.1, f32[256,1024]{1,0:T(8,128)} %filters_hbm.1, f32[1,1024]{1,0:T(1,128)} %bitcast.1, bf16[2,2,512,256]{3,2,1,0:T(8,128)(2,1)} %constant.6.clone.forward_hbm, ...), custom_call_target="tpu_custom_call" | custom-call | tf_op jit(solution)/shard_map/pallas_call | solution.py:389
  62.0 1.9 %copy.10 = bf16[256,1024]{1,0:T(8,128)(2,1)} copy(bf16[256,1024]{1,0:T(8,128)(2,1)} %shard_map.82) | data formatting | bytes 1048576
where the time goes:
time: 64.1 us; the launch traced here: 63.9 us
  Pallas kernels  62 us (97%)
  local copies, waits for them, and re-layouts  1.87 us (3%)
    pallas_call x1, Pallas kernels, per_device_fused(): pl.pallas_call(functools.partial(kernel, blocks, chans, parts), out_shape...  62 us
    unnamed x1, local copies, waits for them, and re-layouts  1.87 us

commit v1 on v0

--- a/solution.py
+++ b/solution.py
@@ -13,6 +13,7 @@
 STRIP = 16
 IN_PARTS = 2
 OUT_PARTS = 4
+LAG = 2
 MESH = pl.DeviceIdType.MESH
 
 
@@ -284,23 +285,23 @@
 
         lax.fori_loop(0, chunk // STRIP, body, 0)
 
-    c_copies = []
-    for part in range(parts):
-        undo(part)
+    def back(part, step):
         rows = pl.ds(part * chunk, chunk)
-        c_copies.append([
-            pltpu.make_async_remote_copy(
-                src_ref=y_send.at[ahead(step), rows],
-                dst_ref=causal.at[me, rows],
-                send_sem=c_out.at[part, step],
-                recv_sem=c_in.at[part, step],
-                device_id={"seq": ahead(step)},
-                device_id_type=MESH,
-            )
-            for step in order
-        ])
+        return pltpu.make_async_remote_copy(
+            src_ref=y_send.at[ahead(step), rows],
+            dst_ref=causal.at[me, rows],
+            send_sem=c_out.at[part, step],
+            recv_sem=c_in.at[part, step],
+            device_id={"seq": ahead(step)},
+            device_id_type=MESH,
+        )
+
+    c_copies = [[back(part, step) for step in order] for part in range(parts)]
+
+    def send(part):
         for copy in c_copies[part]:
             copy.start()
+        rows = pl.ds(part * chunk, chunk)
         causal[me, rows] = y_send[me, rows]
 
     def share(source_chan, target, out_sem, in_sem, part):
@@ -344,31 +345,49 @@
 
         lax.fori_loop(0, out.shape[1] // 256, tile, 0)
 
-    def finish(part):
-        f_copies[part].wait_recv()
-        project(part, (across, opposite), True)
-
-    values_copy.wait()
-    gates_copy.wait()
-    w_copy.wait()
-    for part in range(parts):
+    def receive(part):
         for copy in c_copies[part]:
             copy.wait_recv()
         blend(part)
         a_copies[part].start()
         b_copies[part].start()
-        if part >= 1:
-            a_copies[part - 1].wait_recv()
-            f_copies[part - 1].start()
+
+    def forward_on(part):
+        a_copies[part].wait_recv()
+        f_copies[part].start()
+
+    def near(part):
         b_copies[part].wait_recv()
         project(part, (mine, sibling), False)
-        if part >= 1 and part < parts - 1:
-            finish(part - 1)
-    a_copies[parts - 1].wait_recv()
-    f_copies[parts - 1].start()
+
+    def far(part):
+        f_copies[part].wait_recv()
+        project(part, (across, opposite), True)
+
+    values_copy.wait()
+    gates_copy.wait()
+    lag = min(LAG, parts)
+    for part in range(parts):
+        undo(part)
+        if part >= lag:
+            receive(part - lag)
+            if part > lag:
+                forward_on(part - lag - 1)
+        send(part)
+    w_copy.wait()
+    for part in range(parts - lag):
+        near(part)
+    for part in range(parts - lag, parts):
+        receive(part)
+        if part >= 1:
+            forward_on(part - 1)
+        if part >= 2:
+            far(part - 2)
+        near(part)
+    forward_on(parts - 1)
     if parts >= 2:
-        finish(parts - 2)
-    finish(parts - 1)
+        far(parts - 2)
+    far(parts - 1)
     for copies in v_copies + h_copies + c_copies + [a_copies, b_copies, f_copies]:
         for copy in copies:
             copy.wait_send()

time: 64.1 us -> 62.4 us (0.973)
  Pallas kernels: 62 us -> 60.3 us
    pallas_call x1, Pallas kernels: 62 us -> 60.3 us  [per_device_fused(): pl.pallas_call(functools.partial(kernel, blocks, chans, parts), out_shape...]
where the time goes in v1:
time: 62.4 us; the launch traced here: 62.2 us
  Pallas kernels  60.3 us (97%)
  local copies, waits for them, and re-layouts  1.87 us (3%)
    pallas_call x1, Pallas kernels, per_device_fused(): pl.pallas_call(functools.partial(kernel, blocks, chans, parts), out_shape...  60.3 us
    unnamed x1, local copies, waits for them, and re-layouts  1.87 us

profile of v1, /device:TPU:0, one launch (start us, length us, event | category | flops | bytes accessed | tf_op | source)
XLA Modules:
  0.0 62.2 jit_solution(15495225992285763517)
XLA Ops:
  0.0 60.3 %shard_map.82 = bf16[256,1024]{1,0:T(8,128)(2,1)} custom-call(bf16[256,1024]{1,0:T(8,128)(2,1)} %values_hbm.1, bf16[256,1024]{1,0:T(8,128)(2,1)} %gates_hbm.1, f32[256,1024]{1,0:T(8,128)} %filters_hbm.1, f32[1,1024]{1,0:T(1,128)} %bitcast.1, bf16[2,2,512,256]{3,2,1,0:T(8,128)(2,1)} %constant.6.clone.forward_hbm, ...), custom_call_target="tpu_custom_call" | custom-call | tf_op jit(solution)/shard_map/pallas_call | solution.py:408
  60.3 1.9 %copy.10 = bf16[256,1024]{1,0:T(8,128)(2,1)} copy(bf16[256,1024]{1,0:T(8,128)(2,1)} %shard_map.82) | data formatting | bytes 1048576

commit v2 on v1

--- a/solution.py
+++ b/solution.py
@@ -13,7 +13,6 @@
 STRIP = 16
 IN_PARTS = 2
 OUT_PARTS = 4
-LAG = 2
 MESH = pl.DeviceIdType.MESH
 
 
@@ -327,11 +326,11 @@
                 gates[rows, cols].astype(jnp.float32) * (causal[source, rows].astype(jnp.float32) + direct)
             ).astype(jnp.bfloat16)
 
-    def project(part, pair, last):
-        rows = pl.ds(part * chunk, chunk)
+    def project(group, pair, last):
+        rows = pl.ds(group * 2 * chunk, 2 * chunk)
 
         def tile(n, _):
-            cols = pl.ds(pl.multiple_of(n * 256, 256), 256)
+            cols = pl.ds(pl.multiple_of(n * 512, 512), 512)
             total = None
             for which in pair:
                 deep = pl.ds(pl.multiple_of(which * depth, depth), depth)
@@ -343,7 +342,7 @@
                 acc[rows, cols] = total
             return 0
 
-        lax.fori_loop(0, out.shape[1] // 256, tile, 0)
+        lax.fori_loop(0, out.shape[1] // 512, tile, 0)
 
     def receive(part):
         for copy in c_copies[part]:
@@ -356,38 +355,39 @@
         a_copies[part].wait_recv()
         f_copies[part].start()
 
-    def near(part):
-        b_copies[part].wait_recv()
-        project(part, (mine, sibling), False)
-
-    def far(part):
-        f_copies[part].wait_recv()
-        project(part, (across, opposite), True)
+    def near(group):
+        for part in (2 * group, 2 * group + 1):
+            b_copies[part].wait_recv()
+        project(group, (mine, sibling), False)
+
+    def far(group):
+        for part in (2 * group, 2 * group + 1):
+            f_copies[part].wait_recv()
+        project(group, (across, opposite), True)
 
     values_copy.wait()
     gates_copy.wait()
-    lag = min(LAG, parts)
-    for part in range(parts):
-        undo(part)
-        if part >= lag:
-            receive(part - lag)
-            if part > lag:
-                forward_on(part - lag - 1)
-        send(part)
+    undo(0)
+    send(0)
+    undo(1)
+    send(1)
+    undo(2)
+    receive(0)
+    send(2)
+    undo(3)
+    receive(1)
+    forward_on(0)
+    send(3)
     w_copy.wait()
-    for part in range(parts - lag):
-        near(part)
-    for part in range(parts - lag, parts):
-        receive(part)
-        if part >= 1:
-            forward_on(part - 1)
-        if part >= 2:
-            far(part - 2)
-        near(part)
-    forward_on(parts - 1)
-    if parts >= 2:
-        far(parts - 2)
-    far(parts - 1)
+    near(0)
+    receive(2)
+    forward_on(1)
+    far(0)
+    receive(3)
+    forward_on(2)
+    near(1)
+    forward_on(3)
+    far(1)
     for copies in v_copies + h_copies + c_copies + [a_copies, b_copies, f_copies]:
         for copy in copies:
             copy.wait_send()
@@ -445,7 +445,7 @@
     block, width = values.shape
     fits = (
         width == blocks * LANES and chans == 4 and blocks % 2 == 0 and blocks <= 16
-        and block % 256 == 0 and block <= 512 and w_out.shape[1] % 256 == 0
+        and block % 256 == 0 and block <= 512 and w_out.shape[1] % 512 == 0
     )
     if fits:
         return per_device_fused(blocks, chans, values, gates, filters, skip, w_out)

time: 62.4 us -> 61.2 us (0.981); the launches traced: 62.2 us -> 60.2 us
  Pallas kernels: 60.3 us -> 58.3 us
    pallas_call x1, Pallas kernels: 60.3 us -> 58.3 us  [per_device_fused(): pl.pallas_call(functools.partial(kernel, blocks, chans, parts), out_shape...]
where the time goes in v2:
time: 61.2 us; the launch traced here: 60.2 us
  Pallas kernels  58.3 us (95%)
  local copies, waits for them, and re-layouts  1.87 us (3%)
    pallas_call x1, Pallas kernels, per_device_fused(): pl.pallas_call(functools.partial(kernel, blocks, chans, parts), out_shape...  58.3 us
    unnamed x1, local copies, waits for them, and re-layouts  1.87 us

profile of v2, /device:TPU:0, one launch (start us, length us, event | category | flops | bytes accessed | tf_op | source)
XLA Modules:
  0.0 60.2 jit_solution(297773732200410981)
XLA Ops:
  0.0 58.3 %shard_map.82 = bf16[256,1024]{1,0:T(8,128)(2,1)} custom-call(bf16[256,1024]{1,0:T(8,128)(2,1)} %values_hbm.1, bf16[256,1024]{1,0:T(8,128)(2,1)} %gates_hbm.1, f32[256,1024]{1,0:T(8,128)} %filters_hbm.1, f32[1,1024]{1,0:T(1,128)} %bitcast.1, bf16[2,2,512,256]{3,2,1,0:T(8,128)(2,1)} %constant.6.clone.forward_hbm, ...), custom_call_target="tpu_custom_call" | custom-call | tf_op jit(solution)/shard_map/pallas_call | solution.py:408
  58.3 1.9 %copy.10 = bf16[256,1024]{1,0:T(8,128)(2,1)} copy(bf16[256,1024]{1,0:T(8,128)(2,1)} %shard_map.82) | data formatting | bytes 1048576
